TPU v7x, 256 devices: a whole 4x4x8 slice. The times are simulated.
256 devices in a mesh: row: 32 (over z_hi, y, core), col: 8 (over z_lo, x).
Axes of the slice: x: 4, y: 4, z: 8 (z_hi: 4, z_lo: 2; z = z_hi * 2 + z_lo), core: 2. Of those that a mesh axis runs over, the one named last changes fastest.
Arguments:
- known_inverse: float32 [20480, 20480], P('row', 'col'), may hold values from -1.7818667 to 1.7818667, as said below
- first_panel: float32 [20480, 512], P('col', 'row'), may hold values from -1.25 to 1.25
- second_panel: float32 [20480, 512], P('col', 'row'), may hold values from -1.25 to 1.25
- coupling: float32 [512, 512], replicated, may hold values from -0.25 to 0.25
- first_diag: float32 [512, 512], replicated, may hold values from -6 to 6
- second_diag: float32 [512, 512], replicated, may hold values from -6 to 6
- first_present: int32 [160], replicated, may hold values 0 or 1
- second_present: int32 [160], replicated, may hold values 0 or 1
Outputs:
- first_block: float32 [20480, 512], P(('row', 'col'))
- first_inverse_diag: float32 [512, 512], P(None, 'col')
- second_block: float32 [20480, 512], P(('row', 'col'))
- second_cross: float32 [512, 512], P(None, 'col')
- second_inverse_diag: float32 [512, 512], P(None, 'col')
Inputs may be any that keep to these rules, and one draw needn't show every extreme that they name: known_inverse is exactly symmetric.
All inputs are finite; a program needn't handle non-finite values.
Results may differ from a plain program's by a relative error of at most 0.000098.
Values sent between devices are 32-bit elements; how exact they have to be, the bound alone decides.
A program may use at most 64 MiB of HBM per device.

v0:
```python
import jax
import jax.numpy as jnp
from jax import lax
from jax.sharding import PartitionSpec as P

BLK = 128


def spread(block, axis, holder):
    block = jnp.where(lax.axis_index(axis) == holder, block, jnp.zeros_like(block))
    return lax.psum(block, axis)


def product(left, right):
    return jnp.dot(left, right, precision=lax.Precision.HIGHEST, preferred_element_type=jnp.float32)


def transposed(left, right):
    return lax.dot_general(
        left,
        right,
        (((0,), (0,)), ((), ())),
        precision=lax.Precision.HIGHEST,
        preferred_element_type=jnp.float32,
    )


def masked(panel, present, col_index):
    row_total, col_total = panel.shape
    blocks = row_total // BLK
    local = lax.dynamic_slice_in_dim(present, col_index * blocks, blocks)
    shaped = panel.reshape(blocks, BLK, col_total) * local.astype(jnp.float32)[:, None, None]
    return shaped.reshape(row_total, col_total)


def piece_products(known_inverse, column_one, column_two, piece_one, piece_two, coupling):
    first_block = -lax.psum_scatter(
        product(known_inverse, column_one), "col", scatter_dimension=0, tiled=True
    )
    reached = lax.psum_scatter(
        product(known_inverse, column_two), "col", scatter_dimension=0, tiled=True
    )
    first_partial = transposed(piece_one, first_block)
    second_block = -(reached + product(first_block, coupling))
    cross_partial = transposed(first_block, piece_two)
    diag_partial = transposed(piece_two, second_block)
    return (first_block, second_block, first_partial, cross_partial, diag_partial)


def on_device(
    known_inverse,
    first_panel,
    second_panel,
    coupling,
    first_diag,
    second_diag,
    first_present,
    second_present,
):
    col_count = lax.axis_size("col")
    row_index = lax.axis_index("row")
    col_index = lax.axis_index("col")
    local_one = masked(first_panel, first_present, col_index)
    local_two = masked(second_panel, second_present, col_index)
    column_one, column_two = (
        lax.all_gather(local_one, "row", axis=1, tiled=True),
        lax.all_gather(local_two, "row", axis=1, tiled=True),
    )
    band_rows = known_inverse.shape[0]
    block_cols = known_inverse.shape[1]
    piece_rows = band_rows // col_count
    width_total = coupling.shape[0]
    owner = row_index * band_rows // block_cols
    offset = row_index * band_rows % block_cols
    own_start = col_index * piece_rows
    band_one = lax.dynamic_slice_in_dim(column_one, offset, band_rows)
    band_two = lax.dynamic_slice_in_dim(column_two, offset, band_rows)
    band_one, band_two = (spread(band_one, "col", owner), spread(band_two, "col", owner))
    piece_one = lax.dynamic_slice_in_dim(band_one, own_start, piece_rows)
    piece_two = lax.dynamic_slice_in_dim(band_two, own_start, piece_rows)
    first_block, second_block, first_partial, cross_partial, diag_partial = piece_products(
        known_inverse, column_one, column_two, piece_one, piece_two, coupling
    )
    col_width = width_total // col_count
    col_start = col_index * col_width
    first_sum = lax.psum(first_partial, ("row", "col"))
    first_inverse_diag = first_diag - first_sum
    cross_sum, diag_sum = lax.psum((cross_partial, diag_partial), ("row", "col"))
    second_cross = -(cross_sum + product(first_inverse_diag, coupling))
    second_inverse_diag = second_diag - diag_sum - transposed(coupling, second_cross)
    first_out = lax.dynamic_slice_in_dim(first_inverse_diag, col_start, col_width, 1)
    cross_out = lax.dynamic_slice_in_dim(second_cross, col_start, col_width, 1)
    second_out = lax.dynamic_slice_in_dim(second_inverse_diag, col_start, col_width, 1)
    return (first_block, first_out, second_block, cross_out, second_out)


def solution(mesh):
    in_specs = (P("row", "col"), P("col", "row"), P("col", "row"), P(), P(), P(), P(), P())
    out_specs = (
        P(("row", "col"), None),
        P(None, "col"),
        P(("row", "col"), None),
        P(None, "col"),
        P(None, "col"),
    )
    return jax.shard_map(
        on_device, mesh=mesh, in_specs=in_specs, out_specs=out_specs, check_vma=False
    )
```

profile of v0, /device:TPU:2, one launch (start us, length us, event | category | flops | bytes accessed | tf_op | source)
XLA Modules:
  0.0 611.4 jit_solution(1774505497310201889)
XLA Ops:
  8.2 1.6 broadcast_multiply_fusion.1
  9.9 1.6 broadcast_multiply_fusion
  11.6 66.8 %all-gather.3.cloned.1.call-done = f32[2560,512]{0,1:T(8,128)} async-done(((f32[2560,16]{0,1:T(8,128)}), f32[2560,512]{0,1:T(8,128)}) %all-gather.3.cloned.1.call-update) | async-done | bytes 5242896 | tf_op jit(solution)/shard_map/all_gather | solution.py:66
  78.4 15.7 %convolution_bitcast_fusion.1 = f32[640,512]{0,1:T(8,128)S(1)} fusion(f32[2560,512]{0,1:T(8,128)} %all-gather.3.cloned.1.call-done, f32[640,2560]{1,0:T(8,128)} %param.8), kind=kOutput, calls=%fused_computation.1 | convolution fusion | flops 10066329600 | bytes 13107200 | tf_op jit(solution)/shard_map/dot_general | solution.py:15
  94.1 1.5 copy.27
  95.7 2.9 dynamic-slice_select_fusion.1
  98.6 45.1 %all-gather.5.cloned.1.call-done = f32[2560,512]{0,1:T(8,128)} async-done(((f32[2560,16]{0,1:T(8,128)}), f32[2560,512]{0,1:T(8,128)}) %all-gather.5.cloned.1.call-update) | async-done | bytes 5242896 | tf_op jit(solution)/shard_map/all_gather | solution.py:67
  143.7 3.0 dynamic-slice_select_fusion
  146.9 15.7 %convolution_bitcast_fusion = f32[640,512]{0,1:T(8,128)S(1)} fusion(f32[2560,512]{0,1:T(8,128)} %all-gather.5.cloned.1.call-done, f32[640,2560]{1,0:T(8,128)} %param.8), kind=kOutput, calls=%fused_computation | convolution fusion | flops 10066329600 | bytes 13107200 | tf_op jit(solution)/shard_map/dot_general | solution.py:15
  162.6 1.5 copy.29
  164.4 19.8 %reduce-scatter.7.cloned.1.call-done = f32[80,512]{1,0:T(8,128)} async-done(((f32[640,512]{1,0:T(8,128)}), f32[80,512]{1,0:T(8,128)}) %reduce-scatter.7.cloned.1.call-update) | async-done | bytes 163856
  184.2 1.0 copy.28
  185.3 92.8 %all-reduce.7.cloned.1.call-done = (f32[640,512]{0,1:T(8,128)}, f32[640,512]{0,1:T(8,128)}) async-done(((f32[640,512]{0,1:T(8,128)}, f32[640,512]{0,1:T(8,128)}), (f32[640,512]{0,1:T(8,128)}, f32[640,512]{0,1:T(8,128)})) %all-reduce.7.cloned.1.call-update) | async-done | bytes 2621456 | tf_op jit(solution)/shard_map/psum | solution.py:11
  278.0 3.1 fusion.2
  281.2 3.1 fusion.6
  284.3 37.2 %reduce-scatter.9.cloned.1.call-done = f32[80,512]{1,0:T(8,128)} async-done(((f32[640,512]{1,0:T(8,128)}), f32[80,512]{1,0:T(8,128)}) %reduce-scatter.9.cloned.1.call-update) | async-done | bytes 163856 | tf_op jit(solution)/shard_map/reduce_scatter | solution.py:40
  321.5 1.6 fusion.1
  323.2 3.2 fusion.4
  326.4 1.2 constant_dynamic-slice_fusion
  328.5 267.3 %all-reduce.5.cloned.1.call-done = (f32[512,512]{1,0:T(8,128)}, f32[512,512]{1,0:T(8,128)}, f32[512,512]{0,1:T(8,128)}) async-done(((f32[512,512]{1,0:T(8,128)}, f32[512,512]{1,0:T(8,128)}, f32[512,512]{0,1:T(8,128)}), (f32[512,512]{1,0:T(8,128)}, f32[512,512]{1,0:T(8,128)}, f32[512,512]{0,1:T(8,128)})) %all-reduce.5.cloned.1.call-update) | async-done | bytes 3145744 | tf_op jit(solution)/shard_map/psum | solution.py:86
  595.9 1.5 sub.14
  597.5 1.8 fusion
  599.5 1.8 convolution_bitcast_fusion.2
  602.9 1.6 dynamic-slice_subtract_fusion
  (30 shorter events, 4.5 us)
Async XLA Ops:
  7.2 314.3 %copy-start = (f32[512,512]{1,0:T(8,128)S(1)}, f32[512,512]{1,0:T(8,128)}, u32[]{:S(2)}) copy-start(f32[512,512]{1,0:T(8,128)} %param.11) | copy-start | bytes 3145732
  7.2 71.2 %all-gather.3.cloned.1.call-start = ((), (), s32[]{:S(2)}) async-start(), calls=%async_computation.2 | async-start | bytes 5406720 | tf_op jit(solution)/shard_map/all_gather | solution.py:66
  9.8 133.9 %all-gather.5.cloned.1.call-start = ((), (), s32[]{:S(2)}) async-start(), calls=%async_computation.3 | async-start | bytes 5406720 | tf_op jit(solution)/shard_map/all_gather | solution.py:67
  11.5 172.7 %reduce-scatter.7.cloned.1.call-start = ((), (), s32[]{:S(2)}) async-start(), calls=%async_computation.4 | async-start | bytes 1474560
  95.6 182.4 %all-reduce.7.cloned.1.call-start = ((), (), s32[]{:S(2)}) async-start(), calls=%async_computation.7 | async-start | bytes 5242880 | tf_op jit(solution)/shard_map/psum | solution.py:11
  146.7 174.8 %reduce-scatter.9.cloned.1.call-start = ((), (), s32[]{:S(2)}) async-start(), calls=%async_computation.5 | async-start | bytes 1474560 | tf_op jit(solution)/shard_map/reduce_scatter | solution.py:40
  164.1 431.7 %all-reduce.5.cloned.1.call-start = ((), (), s32[]{:S(2)}) async-start(), calls=%async_computation.6 | async-start | bytes 6291456 | tf_op jit(solution)/shard_map/psum | solution.py:86
  323.1 3.2 copy-start.3
  326.4 269.5 %copy-start.1 = (f32[512,512]{1,0:T(8,128)S(1)}, f32[512,512]{1,0:T(8,128)}, u32[]{:S(2)}) copy-start(f32[512,512]{1,0:T(8,128)} %param.12) | copy-start | bytes 3145732
  595.9 1.7 copy-start.2
Sparse Core Ops, SparseCore 0:
  11.1 67.2 all-gather.2
  81.5 62.1 all-gather.4
  146.2 37.9 reduce-scatter.6
  186.8 91.2 all-reduce.6
  280.4 41.0 reduce-scatter.8
  327.1 268.6 all-reduce.4
where the time goes:
time: 612 us; the launch traced here: 611 us
  waiting for transfers between devices  529 us (86%)
  matrix products  46.2 us (8%)
  between operations  14.3 us (2%)
  other arithmetic  13.1 us (2%)
  local copies, waits for them, and re-layouts  8.01 us (1%)
    psum x1, waiting for transfers between devices, on_device(): first_sum = lax.psum(first_partial, ('row', 'col'))  267 us
    psum x1, waiting for transfers between devices, spread(): return lax.psum(block, axis)  92.8 us
    all_gather x1, waiting for transfers between devices, on_device(): lax.all_gather(local_one, 'row', axis=1, tiled=True)  66.8 us
    all_gather x1, waiting for transfers between devices, on_device(): lax.all_gather(local_two, 'row', axis=1, tiled=True)  45.1 us
    reduce_scatter x1, waiting for transfers between devices, piece_products(): lax.psum_scatter(product(known_inverse, column_two), 'col', scatter_dimen...  37.2 us
    dot_general x4, matrix products, product(): jnp.dot(left, right, precision=lax.Precision.HIGHEST, preferred_element_t...  35 us
    unnamed x7, waiting for transfers between devices  19.9 us
  transfers between devices with their start and end apart: 6, of which 6 were waited for; matrix products, arithmetic and copies ran while one was open for 8% of the time, Pallas kernels for 0%

commit v1 on v0

--- a/solution.py
+++ b/solution.py
@@ -83,7 +83,7 @@
     )
     col_width = width_total // col_count
     col_start = col_index * col_width
-    first_sum = lax.psum(first_partial, ("row", "col"))
+    first_sum = lax.psum(lax.psum(first_partial, "row"), "col")
     first_inverse_diag = first_diag - first_sum
     cross_sum, diag_sum = lax.psum((cross_partial, diag_partial), ("row", "col"))
     second_cross = -(cross_sum + product(first_inverse_diag, coupling))

time: 612 us -> 999 us (1.63)
  waiting for transfers between devices: 529 us -> 915 us
    psum x1 -> x3, waiting for transfers between devices: 267 us -> 621 us  [the longest x2 360 us: on_device(): first_sum = lax.psum(lax.psum(first_partial, 'row'), 'col')]
    all_gather x1, waiting for transfers between devices: 45.1 us -> 65.3 us  [on_device(): lax.all_gather(local_two, 'row', axis=1, tiled=True)]
    unnamed x7 -> x9, waiting for transfers between devices: 19.9 us -> 33.5 us
  transfers between devices with their start and end apart: 6 -> 8, of which waited for: 6 -> 8; matrix products, arithmetic and copies ran while one was open for 8% -> 3% of each run, Pallas kernels for 0% -> 0%
where the time goes in v1:
time: 999 us; the launch traced here: 998 us
  waiting for transfers between devices  915 us (92%)
  matrix products  47.3 us (5%)
  between operations  14.3 us (1%)
  other arithmetic  12.1 us (1%)
    psum x2, waiting for transfers between devices, on_device(): first_sum = lax.psum(lax.psum(first_partial, 'row'), 'col')  360 us
    psum x1, waiting for transfers between devices, on_device(): lax.psum((cross_partial, diag_partial), ('row', 'col'))  261 us
    psum x1, waiting for transfers between devices, spread(): return lax.psum(block, axis)  85.1 us
    all_gather x1, waiting for transfers between devices, on_device(): lax.all_gather(local_one, 'row', axis=1, tiled=True)  68.5 us
    all_gather x1, waiting for transfers between devices, on_device(): lax.all_gather(local_two, 'row', axis=1, tiled=True)  65.3 us
    reduce_scatter x1, waiting for transfers between devices, piece_products(): lax.psum_scatter(product(known_inverse, column_two), 'col', scatter_dimen...  41.8 us
    dot_general x4, matrix products, product(): jnp.dot(left, right, precision=lax.Precision.HIGHEST, preferred_element_t...  36.2 us
    unnamed x9, waiting for transfers between devices  33.5 us
  transfers between devices with their start and end apart: 8, of which 8 were waited for; matrix products, arithmetic and copies ran while one was open for 3% of the time, Pallas kernels for 0%

profile of v1, /device:TPU:2, one launch (start us, length us, event | category | flops | bytes accessed | tf_op | source)
XLA Modules:
  0.0 998.1 jit_solution(1562031844266467298)
XLA Ops:
  8.2 1.6 broadcast_multiply_fusion.1
  9.8 68.5 %all-gather.3.cloned.1.call-done = f32[2560,512]{0,1:T(8,128)} async-done(((f32[2560,16]{0,1:T(8,128)}), f32[2560,512]{0,1:T(8,128)}) %all-gather.3.cloned.1.call-update) | async-done | bytes 5242896 | tf_op jit(solution)/shard_map/all_gather | solution.py:66
  78.4 15.7 %convolution_bitcast_fusion.1 = f32[640,512]{0,1:T(8,128)S(1)} fusion(f32[2560,512]{0,1:T(8,128)} %all-gather.3.cloned.1.call-done, f32[640,2560]{1,0:T(8,128)} %param.8), kind=kOutput, calls=%fused_computation.1 | convolution fusion | flops 10066329600 | bytes 13107200 | tf_op jit(solution)/shard_map/dot_general | solution.py:15
  94.1 1.5 copy.27
  95.7 3.0 dynamic-slice_select_fusion.1
  100.3 33.4 %reduce-scatter.7.cloned.1.call-done = f32[80,512]{1,0:T(8,128)} async-done(((f32[640,512]{1,0:T(8,128)}), f32[80,512]{1,0:T(8,128)}) %reduce-scatter.7.cloned.1.call-update) | async-done | bytes 163856
  134.7 85.1 %all-reduce.7.cloned.1.call-done = f32[640,512]{0,1:T(8,128)} async-done(((f32[640,512]{0,1:T(8,128)}), f32[640,512]{0,1:T(8,128)}) %all-reduce.7.cloned.1.call-update) | async-done | bytes 1310736 | tf_op jit(solution)/shard_map/psum | solution.py:11
  219.8 3.0 fusion.2
  223.1 65.3 %all-gather.5.cloned.1.call-done = f32[2560,512]{0,1:T(8,128)} async-done(((f32[2560,16]{0,1:T(8,128)}), f32[2560,512]{0,1:T(8,128)}) %all-gather.5.cloned.1.call-update) | async-done | bytes 5242896 | tf_op jit(solution)/shard_map/all_gather | solution.py:67
  288.4 15.7 %convolution_bitcast_fusion = f32[640,512]{0,1:T(8,128)S(1)} fusion(f32[2560,512]{0,1:T(8,128)} %all-gather.5.cloned.1.call-done, f32[640,2560]{1,0:T(8,128)} %param.8), kind=kOutput, calls=%fused_computation | convolution fusion | flops 10066329600 | bytes 13107200 | tf_op jit(solution)/shard_map/dot_general | solution.py:15
  304.2 1.5 copy.29
  305.7 2.9 dynamic-slice_select_fusion
  308.6 269.4 %all-reduce.9.cloned.1.call-done = f32[512,512]{1,0:T(8,128)} async-done(((f32[512,512]{1,0:T(8,128)}), f32[512,512]{1,0:T(8,128)}) %all-reduce.9.cloned.1.call-update) | async-done | bytes 1048592 | tf_op jit(solution)/shard_map/psum | solution.py:86
  578.4 41.8 %reduce-scatter.9.cloned.1.call-done = f32[80,512]{1,0:T(8,128)} async-done(((f32[640,512]{1,0:T(8,128)}), f32[80,512]{1,0:T(8,128)}) %reduce-scatter.9.cloned.1.call-update) | async-done | bytes 163856 | tf_op jit(solution)/shard_map/reduce_scatter | solution.py:40
  620.2 1.6 fusion.1
  621.8 90.3 %all-reduce.13.cloned.1.call-done = (f32[512,512]{1,0:T(8,128)}, f32[640,512]{0,1:T(8,128)}) async-done(((f32[512,512]{1,0:T(8,128)}, f32[640,512]{0,1:T(8,128)}), (f32[512,512]{1,0:T(8,128)}, f32[640,512]{0,1:T(8,128)})) %all-reduce.13.cloned.1.call-update) | async-done | bytes 2359312 | tf_op jit(solution)/shard_map/psum | solution.py:86
  712.1 3.1 fusion.6
  715.2 3.1 fusion.4
  718.4 1.2 constant_dynamic-slice_fusion
  720.5 1.4 sub.14
  722.9 261.0 %all-reduce.11.cloned.1.call-done = (f32[512,512]{1,0:T(8,128)}, f32[512,512]{0,1:T(8,128)}) async-done(((f32[512,512]{1,0:T(8,128)}, f32[512,512]{0,1:T(8,128)}), (f32[512,512]{1,0:T(8,128)}, f32[512,512]{0,1:T(8,128)})) %all-reduce.11.cloned.1.call-update) | async-done | bytes 2097168 | tf_op jit(solution)/shard_map/psum | solution.py:88
  983.8 3.1 fusion
  986.9 1.8 convolution_bitcast_fusion.2
  989.7 1.6 dynamic-slice_subtract_fusion
  (36 shorter events, 7.1 us)
Async XLA Ops:
  7.2 613.0 %copy-start = (f32[512,512]{1,0:T(8,128)S(1)}, f32[512,512]{1,0:T(8,128)}, u32[]{:S(2)}) copy-start(f32[512,512]{1,0:T(8,128)} %param.11) | copy-start | bytes 3145732
  7.2 71.2 %all-gather.3.cloned.1.call-start = ((), (), s32[]{:S(2)}) async-start(), calls=%async_computation.2 | async-start | bytes 5406720 | tf_op jit(solution)/shard_map/all_gather | solution.py:66
  9.8 123.9 %reduce-scatter.7.cloned.1.call-start = ((), (), s32[]{:S(2)}) async-start(), calls=%async_computation.6 | async-start | bytes 1474560
  95.6 124.2 %all-reduce.7.cloned.1.call-start = ((), (), s32[]{:S(2)}) async-start(), calls=%async_computation.3 | async-start | bytes 2621440 | tf_op jit(solution)/shard_map/psum | solution.py:11
  98.7 0.9 copy-start.3
  98.7 189.7 %all-gather.5.cloned.1.call-start = ((), (), s32[]{:S(2)}) async-start(), calls=%async_computation.5 | async-start | bytes 5406720 | tf_op jit(solution)/shard_map/all_gather | solution.py:67
  100.3 477.8 %all-reduce.9.cloned.1.call-start = ((), (), s32[]{:S(2)}) async-start(), calls=%async_computation.4 | async-start | bytes 2097152 | tf_op jit(solution)/shard_map/psum | solution.py:86
  222.9 397.3 %reduce-scatter.9.cloned.1.call-start = ((), (), s32[]{:S(2)}) async-start(), calls=%async_computation.7 | async-start | bytes 1474560 | tf_op jit(solution)/shard_map/reduce_scatter | solution.py:40
  305.7 406.5 %all-reduce.13.cloned.1.call-start = ((), (), s32[]{:S(2)}) async-start(), calls=%async_computation.9 | async-start | bytes 4718592 | tf_op jit(solution)/shard_map/psum | solution.py:86
  578.1 405.7 %all-reduce.11.cloned.1.call-start = ((), (), s32[]{:S(2)}) async-start(), calls=%async_computation.8 | async-start | bytes 4194304 | tf_op jit(solution)/shard_map/psum | solution.py:88
  621.8 96.6 %copy-start.2 = (f32[80,512]{1,0:T(8,128)}, f32[80,512]{1,0:T(8,128)S(1)}, u32[]{:S(2)}) copy-start(f32[80,512]{1,0:T(8,128)S(1)} %fusion.1) | copy-start | bytes 491524
  718.4 2.1 copy-start.1
Sparse Core Ops, SparseCore 0:
  11.1 67.2 all-gather.2
  95.7 37.9 reduce-scatter.6
  136.4 83.4 all-reduce.6
  222.8 65.6 all-gather.4
  290.9 287.1 all-reduce.8
  580.5 39.6 reduce-scatter.8
  622.9 89.1 all-reduce.12
  718.5 265.2 all-reduce.10
